TPU v7x, 128 devices: a whole 4x4x4 slice. The times are simulated.
128 devices in a mesh: wide: 8 (over z_hi, y), narrow: 16 (over x, z_lo, core).
Axes of the slice: x: 4, y: 4, z: 4 (z_hi: 2, z_lo: 2; z = z_hi * 2 + z_lo), core: 2. Of those that a mesh axis runs over, the one named last changes fastest.
Arguments:
- hinv_start: float32 [16384, 16384], P('wide', 'narrow'), as said below
- weights: bfloat16 [2048, 16384], P('narrow', 'wide'), may hold values from -6 to 6
- removed: int32 [1, 512], replicated, may hold values from 0 to 16383, as said below
Outputs:
- hinv_out: float32 [16384, 16384], P('wide', 'narrow')
- weights_out: bfloat16 [2048, 16384], P('narrow', 'wide')
Inputs may be any that keep to these rules, and one draw needn't show every extreme that they name: `removed`: all 1 x 512 indices are distinct; 0 and 16383 are always among them. `hinv_start`: symmetric and positive definite.
All inputs are finite; a program needn't handle non-finite values. Where the computation divides by a largest or mean magnitude, that divisor is 1e-20 or more.
Results may differ from a plain program's by a relative error of at most 0.0036.
Values may be sent and summed in bfloat16 or wider, within the bound.
No kernel may reach another device: no remote copies, remote signals or barrier semaphores. Data moves between devices by JAX's collectives and lax.ppermute only.
A program may use at most 128 MiB of HBM per device.

v0:
```python
import jax
import jax.numpy as jnp
from jax import lax
from jax.sharding import PartitionSpec as P

ITERS = 8


def from_root(x, axis, root):
    mine = lax.axis_index(axis) == root
    return lax.psum(jnp.where(mine, x, jnp.zeros_like(x)), axis)


def per_device(hinv_start, weights, removed):
    wide_count = lax.axis_size("wide")
    narrow_count = lax.axis_size("narrow")
    row_count, col_count = hinv_start.shape
    row_start = lax.axis_index("wide") * row_count
    col_start = lax.axis_index("narrow") * col_count
    blocks_each = narrow_count // wide_count
    block = removed.shape[1]
    identity = jnp.eye(block, dtype=jnp.float32)
    hess = hinv_start
    wmat = weights
    column_ids = row_start + jnp.arange(row_count, dtype=jnp.int32)
    picked = removed[0]
    row_hit = (picked >= row_start) & (picked < row_start + row_count)
    row_local = jnp.clip(picked - row_start, 0, row_count - 1)
    col_hit = (picked >= col_start) & (picked < col_start + col_count)
    col_local = jnp.clip(picked - col_start, 0, col_count - 1)
    row_part = jnp.where(row_hit[:, None], jnp.take(hess, row_local, axis=0), 0.0)
    weight_part = jnp.where(
        row_hit[None, :], jnp.take(wmat, row_local, axis=1).astype(jnp.float32), 0.0
    )
    rows_here, chosen = lax.psum((row_part, weight_part), "wide")
    pivot_part = jnp.where(col_hit[None, :], jnp.take(rows_here, col_local, axis=1), 0.0)
    pivot = lax.psum(pivot_part, "narrow")
    first_root = lax.axis_index("wide") * blocks_each
    col_part = jnp.where(col_hit[None, :], jnp.take(hess, col_local, axis=1), 0.0)
    columns = lax.psum(col_part, "narrow")
    rounded = rows_here.astype(jnp.bfloat16)
    pieces = []
    for offset in range(blocks_each):
        pieces.append(from_root(rounded, "narrow", first_root + offset))
    panel = jnp.concatenate(pieces, axis=1)
    scale = 1.0 / jnp.max(jnp.sum(jnp.abs(pivot), axis=1))
    start_guess = identity * scale
    width = block // wide_count
    own = lax.axis_index("wide") * width
    eye_cols = lax.dynamic_slice_in_dim(identity, own, width, 1)
    current = lax.dynamic_slice_in_dim(start_guess, own, width, 1)
    for turn in range(ITERS):
        right = 2.0 * eye_cols - jnp.dot(pivot, current, precision=lax.Precision.HIGHEST)

        def add_wide(total, piece, start, right=right):
            return jnp.dot(piece, right, precision=lax.Precision.HIGHEST)

        current = add_wide(
            jnp.zeros((block, width), jnp.float32),
            lax.all_gather(current, "wide", axis=1, tiled=True),
            jnp.int32(0),
        )
    inverse = lax.all_gather(current, "wide", axis=1, tiled=True)
    gain = jnp.dot(chosen, inverse, precision=lax.Precision.HIGHEST).astype(jnp.bfloat16)
    delta = jnp.dot(gain, panel, preferred_element_type=jnp.float32)
    cleared = jnp.any(picked[:, None] == column_ids[None, :], axis=0)
    wmat = jnp.where(cleared[None, :], 0.0, wmat.astype(jnp.float32) - delta).astype(jnp.bfloat16)
    inner_rows = jnp.dot(inverse, rows_here, precision=lax.Precision.HIGHEST)
    hess = hess - jnp.dot(columns, inner_rows, precision=lax.Precision.HIGHEST)
    return (hess, wmat)


def solution(mesh):
    return jax.shard_map(
        per_device,
        mesh=mesh,
        in_specs=(P("wide", "narrow"), P("narrow", "wide"), P()),
        out_specs=(P("wide", "narrow"), P("narrow", "wide")),
        check_vma=False,
    )
```

profile of v0, /device:TPU:0, one launch (start us, length us, event | category | flops | bytes accessed | tf_op | source)
XLA Modules:
  0.0 836.1 jit_solution(4168252360116877082)
XLA Ops:
  12.0 6.2 gather_fusion.1
  20.9 9.1 %copy.15 = f32[2048,1024]{0,1:T(8,128)} copy(f32[2048,1024]{1,0:T(8,128)} %param.3) | data formatting | bytes 16777216 | tf_op args[0]
  30.0 9.0 %gather_fusion = f32[512,2048]{1,0:T(8,128)} fusion(f32[2048,1024]{0,1:T(8,128)} %copy.15, s32[1024]{0:T(1024)S(1)} %pad_clamp_fusion.1), kind=kCustom, calls=%fused_computation | custom fusion | bytes 8390656 | tf_op jit(solution)/shard_map/jit(_take)/gather | solution.py:39
  39.0 4.7 select_bitcast_fusion
  43.7 73.7 %all-reduce.9.cloned.1.call-done = (f32[512,1024]{1,0:T(8,128)}, f32[128,512]{0,1:T(8,128)}) async-done(((f32[512,1024]{1,0:T(8,128)}, f32[128,512]{0,1:T(8,128)}), (f32[512,1024]{1,0:T(8,128)}, f32[128,512]{0,1:T(8,128)})) %all-reduce.9.cloned.1.call-update) | async-done | bytes 2359312 | tf_op jit(solution)/shard_map/psum | solution.py:35
  122.7 135.8 %all-reduce.7.cloned.1.call-done = (f32[2048,512]{0,1:T(8,128)}, f32[512,512]{1,0:T(8,128)}) async-done(((f32[2048,512]{0,1:T(8,128)}, f32[512,512]{1,0:T(8,128)}), (f32[2048,512]{0,1:T(8,128)}, f32[512,512]{1,0:T(8,128)})) %all-reduce.7.cloned.1.call-update) | async-done | bytes 5242896 | tf_op jit(solution)/shard_map/psum | solution.py:40
  262.0 2.4 convolution_subtract_fusion.9
  264.4 45.5 %all-gather.10.cloned.1.call-done = f32[512,512]{0,1:T(8,128)} async-done(((f32[512,64]{0,1:T(8,128)}), f32[512,512]{0,1:T(8,128)}) %all-gather.10.cloned.1.call-update) | async-done | bytes 1048592 | tf_op jit(solution)/shard_map/all_gather | solution.py:60
  309.9 2.7 fusion.7
  312.7 2.1 convolution_subtract_fusion.8
  314.7 44.0 %all-gather.12.cloned.1.call-done = f32[512,512]{0,1:T(8,128)} async-done(((f32[512,64]{0,1:T(8,128)}), f32[512,512]{0,1:T(8,128)}) %all-gather.12.cloned.1.call-update) | async-done | bytes 1048592 | tf_op jit(solution)/shard_map/all_gather | solution.py:60
  358.7 2.7 fusion.8
  363.5 44.0 %all-gather.14.cloned.1.call-done = f32[512,512]{0,1:T(8,128)} async-done(((f32[512,64]{0,1:T(8,128)}), f32[512,512]{0,1:T(8,128)}) %all-gather.14.cloned.1.call-update) | async-done | bytes 1048592 | tf_op jit(solution)/shard_map/all_gather | solution.py:60
  407.5 2.7 fusion.9
  412.5 43.8 %all-gather.16.cloned.1.call-done = f32[512,512]{0,1:T(8,128)} async-done(((f32[512,64]{0,1:T(8,128)}), f32[512,512]{0,1:T(8,128)}) %all-gather.16.cloned.1.call-update) | async-done | bytes 1048592 | tf_op jit(solution)/shard_map/all_gather | solution.py:60
  456.3 2.7 fusion.10
  459.0 2.1 convolution_subtract_fusion.5
  461.1 44.1 %all-gather.18.cloned.1.call-done = f32[512,512]{0,1:T(8,128)} async-done(((f32[512,64]{0,1:T(8,128)}), f32[512,512]{0,1:T(8,128)}) %all-gather.18.cloned.1.call-update) | async-done | bytes 1048592 | tf_op jit(solution)/shard_map/all_gather | solution.py:60
  505.2 2.7 fusion.11
  507.9 2.2 convolution_subtract_fusion.4
  510.1 43.9 %all-gather.20.cloned.1.call-done = f32[512,512]{0,1:T(8,128)} async-done(((f32[512,64]{0,1:T(8,128)}), f32[512,512]{0,1:T(8,128)}) %all-gather.20.cloned.1.call-update) | async-done | bytes 1048592 | tf_op jit(solution)/shard_map/all_gather | solution.py:60
  554.1 2.7 fusion.12
  558.8 44.1 %all-gather.22.cloned.1.call-done = f32[512,512]{0,1:T(8,128)} async-done(((f32[512,64]{0,1:T(8,128)}), f32[512,512]{0,1:T(8,128)}) %all-gather.22.cloned.1.call-update) | async-done | bytes 1048592 | tf_op jit(solution)/shard_map/all_gather | solution.py:60
  602.9 2.7 fusion.13
  607.8 44.0 %all-gather.24.cloned.1.call-done = f32[512,512]{0,1:T(8,128)} async-done(((f32[512,64]{0,1:T(8,128)}), f32[512,512]{0,1:T(8,128)}) %all-gather.24.cloned.1.call-update) | async-done | bytes 1048592 | tf_op jit(solution)/shard_map/all_gather | solution.py:60
  651.7 2.7 fusion.14
  657.0 43.7 %all-gather.26.cloned.1.call-done = f32[512,512]{0,1:T(8,128)} async-done(((f32[512,64]{0,1:T(8,128)}), f32[512,512]{0,1:T(8,128)}) %all-gather.26.cloned.1.call-update) | async-done | bytes 1048592 | tf_op jit(solution)/shard_map/all_gather | solution.py:63
  700.6 2.6 convolution_convert_fusion
  703.2 4.7 fusion.15
  708.0 17.1 %convolution_subtract_fusion = f32[2048,1024]{1,0:T(8,128)} fusion(f32[2048,1024]{1,0:T(8,128)} %param.3, f32[2048,512]{0,1:T(8,128)S(1)} %copy-done.2, f32[512,1024]{1,0:T(8,128)S(1)} %fusion.15), kind=kOutput, calls=%fused_computation.6 | convolution fusion | flops 12886999040 | bytes 23068672 | tf_op jit(solution)/shard_map/dot_general | solution.py:69
  725.0 101.4 %all-reduce.11.cloned.1.call-done = (bf16[512,1024]{1,0:T(8,128)(2,1)}, bf16[512,1024]{1,0:T(8,128)(2,1)}) async-done(((bf16[512,1024]{1,0:T(8,128)(2,1)}, bf16[512,1024]{1,0:T(8,128)(2,1)}), (bf16[512,1024]{1,0:T(8,128)(2,1)}, bf16[512,1024]{1,0:T(8,128)(2,1)})) %all-reduce.11.cloned.1.call-update) | async-done | bytes 2097168 | tf_op jit(solution)/shard_map/psum | solution.py:11
  826.4 2.8 fusion.1
  (60 shorter events, 26.8 us)
Async XLA Ops:
  7.2 110.3 %all-reduce.9.cloned.1.call-start = ((), (), s32[]{:S(2)}) async-start(), calls=%async_computation.10 | async-start | bytes 4718592 | tf_op jit(solution)/shard_map/psum | solution.py:35
  20.8 237.7 %all-reduce.7.cloned.1.call-start = ((), (), s32[]{:S(2)}) async-start(), calls=%async_computation.9 | async-start | bytes 10485760 | tf_op jit(solution)/shard_map/psum | solution.py:40
  122.6 187.4 %all-gather.10.cloned.1.call-start = ((), (), s32[]{:S(2)}) async-start(), calls=%async_computation | async-start | bytes 1179648 | tf_op jit(solution)/shard_map/all_gather | solution.py:60
  258.5 54.2 %copy-start = (f32[512,512]{1,0:T(8,128)S(1)}, f32[512,512]{1,0:T(8,128)}, u32[]{:S(2)}) copy-start(f32[512,512]{1,0:T(8,128)} %get-tuple-element.5) | copy-start | bytes 3145732
  262.0 96.7 %all-gather.12.cloned.1.call-start = ((), (), s32[]{:S(2)}) async-start(), calls=%async_computation.1 | async-start | bytes 1179648 | tf_op jit(solution)/shard_map/all_gather | solution.py:60
  312.6 94.9 %all-gather.14.cloned.1.call-start = ((), (), s32[]{:S(2)}) async-start(), calls=%async_computation.2 | async-start | bytes 1179648 | tf_op jit(solution)/shard_map/all_gather | solution.py:60
  361.4 94.9 %all-gather.16.cloned.1.call-start = ((), (), s32[]{:S(2)}) async-start(), calls=%async_computation.3 | async-start | bytes 1179648 | tf_op jit(solution)/shard_map/all_gather | solution.py:60
  410.2 95.0 %all-gather.18.cloned.1.call-start = ((), (), s32[]{:S(2)}) async-start(), calls=%async_computation.4 | async-start | bytes 1179648 | tf_op jit(solution)/shard_map/all_gather | solution.py:60
  459.0 95.1 %all-gather.20.cloned.1.call-start = ((), (), s32[]{:S(2)}) async-start(), calls=%async_computation.5 | async-start | bytes 1179648 | tf_op jit(solution)/shard_map/all_gather | solution.py:60
  507.9 146.8 %copy-start.1 = (f32[512,1024]{1,0:T(8,128)S(1)}, f32[512,1024]{1,0:T(8,128)}, u32[]{:S(2)}) copy-start(f32[512,1024]{1,0:T(8,128)} %get-tuple-element.6) | copy-start | bytes 6291460
  507.9 95.1 %all-gather.22.cloned.1.call-start = ((), (), s32[]{:S(2)}) async-start(), calls=%async_computation.6 | async-start | bytes 1179648 | tf_op jit(solution)/shard_map/all_gather | solution.py:60
  556.7 95.0 %all-gather.24.cloned.1.call-start = ((), (), s32[]{:S(2)}) async-start(), calls=%async_computation.7 | async-start | bytes 1179648 | tf_op jit(solution)/shard_map/all_gather | solution.py:60
  605.6 95.0 %all-gather.26.cloned.1.call-start = ((), (), s32[]{:S(2)}) async-start(), calls=%async_computation.8 | async-start | bytes 1179648 | tf_op jit(solution)/shard_map/all_gather | solution.py:63
  607.7 48.6 %copy-start.5 = (s32[1,512]{1,0:T(1,128)S(1)}, s32[1,512]{1,0:T(1,128)}, u32[]{:S(2)}) copy-start(s32[1,512]{1,0:T(1,128)} %param.5) | copy-start | bytes 6148
  607.7 92.9 %copy-start.4 = (f32[128,512]{0,1:T(8,128)S(1)}, f32[128,512]{0,1:T(8,128)}, u32[]{:S(2)}) copy-start(f32[128,512]{0,1:T(8,128)} %get-tuple-element.7) | copy-start | bytes 786436
  654.4 172.0 %all-reduce.11.cloned.1.call-start = ((), (), s32[]{:S(2)}) async-start(), calls=%async_computation.11 | async-start | bytes 4194304 | tf_op jit(solution)/shard_map/psum | solution.py:11
  700.6 7.3 copy-start.2
  708.0 118.4 %copy-start.3 = (bf16[128,2048]{1,0:T(8,128)(2,1)S(1)}, bf16[128,2048]{1,0:T(8,128)(2,1)}, u32[]{:S(2)}) copy-start(bf16[128,2048]{1,0:T(8,128)(2,1)} %param.4) | copy-start | bytes 1572868
Sparse Core Ops, SparseCore 0:
  21.0 96.4 all-reduce.8
  122.7 135.7 all-reduce.6
  262.1 47.7 all-gather.9
  312.7 45.9 all-gather.11
  361.5 45.9 all-gather.13
  410.3 45.9 all-gather.15
  459.2 45.9 all-gather.17
  508.1 45.9 all-gather.19
  557.0 45.9 all-gather.21
  605.8 45.9 all-gather.23
  654.6 45.9 all-gather.25
  703.0 123.3 all-reduce.10
where the time goes:
time: 837 us; the launch traced here: 836 us
  waiting for transfers between devices  708 us (85%)
  matrix products  65.4 us (8%)
  local copies, waits for them, and re-layouts  30.9 us (4%)
  other arithmetic  15.7 us (2%)
  between operations  15.1 us (2%)
    all_gather x8, waiting for transfers between devices, per_device(): lax.all_gather(current, 'wide', axis=1, tiled=True)  353 us
    psum x1, waiting for transfers between devices, per_device(): columns = lax.psum(col_part, 'narrow')  136 us
    psum x1, waiting for transfers between devices, from_root(): return lax.psum(jnp.where(mine, x, jnp.zeros_like(x)), axis)  101 us
    psum x1, waiting for transfers between devices, per_device(): rows_here, chosen = lax.psum((row_part, weight_part), 'wide')  73.7 us
    all_gather x1, waiting for transfers between devices, per_device(): inverse = lax.all_gather(current, 'wide', axis=1, tiled=True)  43.7 us
    dot_general x8, matrix products, add_wide(): return jnp.dot(piece, right, precision=lax.Precision.HIGHEST)  21.3 us
    dot_general x1, matrix products, per_device(): hess = hess - jnp.dot(columns, inner_rows, precision=lax.Precision.HIGHEST)  17.1 us
    dot_general x8, matrix products, per_device(): jnp.dot(pivot, current, precision=lax.Precision.HIGHEST)  16.9 us
  transfers between devices with their start and end apart: 12, of which 12 were waited for; matrix products, arithmetic and copies ran while one was open for 8% of the time, Pallas kernels for 0%

commit v1 on v0

--- a/solution.py
+++ b/solution.py
@@ -37,7 +37,8 @@
     pivot = lax.psum(pivot_part, "narrow")
     first_root = lax.axis_index("wide") * blocks_each
     col_part = jnp.where(col_hit[None, :], jnp.take(hess, col_local, axis=1), 0.0)
-    columns = lax.psum(col_part, "narrow")
+    small = lax.all_gather(col_part, "narrow")
+    columns = jnp.sum(small, 0)
     rounded = rows_here.astype(jnp.bfloat16)
     pieces = []
     for offset in range(blocks_each):

time: 837 us -> 1190 us (1.42)
  waiting for transfers between devices: 708 us -> 1030 us
  other arithmetic: 15.7 us -> 38.6 us
    all_gather x0 -> x1, waiting for transfers between devices: none -> 323 us  [per_device(): small = lax.all_gather(col_part, 'narrow')]
    all_gather x1, waiting for transfers between devices: 43.7 us -> 15.2 us  [per_device(): inverse = lax.all_gather(current, 'wide', axis=1, tiled=True)]
    unnamed x0 -> x1, other arithmetic: none -> 23.1 us
    psum x1, waiting for transfers between devices: 73.7 us -> 96.5 us  [per_device(): rows_here, chosen = lax.psum((row_part, weight_part), 'wide')]
    psum x1, waiting for transfers between devices: 101 us -> 123 us  [from_root(): return lax.psum(jnp.where(mine, x, jnp.zeros_like(x)), axis)]
    psum x1, waiting for transfers between devices: 136 us -> 118 us  [per_device(): pivot = lax.psum(pivot_part, 'narrow')]
  transfers between devices with their start and end apart: 12 -> 13, of which waited for: 12 -> 13; matrix products, arithmetic and copies ran while one was open for 8% -> 5% of each run, Pallas kernels for 0% -> 0%
where the time goes in v1:
time: 1190 us
  waiting for transfers between devices  1030 us (87%)
  matrix products  66.2 us (6%)
  other arithmetic  38.6 us (3%)
  local copies, waits for them, and re-layouts  36.7 us (3%)
  between operations  14.7 us (1%)
    all_gather x8, waiting for transfers between devices, per_device(): lax.all_gather(current, 'wide', axis=1, tiled=True)  354 us
    all_gather x1, waiting for transfers between devices, per_device(): small = lax.all_gather(col_part, 'narrow')  323 us
    psum x1, waiting for transfers between devices, from_root(): return lax.psum(jnp.where(mine, x, jnp.zeros_like(x)), axis)  123 us
    psum x1, waiting for transfers between devices, per_device(): pivot = lax.psum(pivot_part, 'narrow')  118 us
    psum x1, waiting for transfers between devices, per_device(): rows_here, chosen = lax.psum((row_part, weight_part), 'wide')  96.5 us
  transfers between devices with their start and end apart: 13, of which 13 were waited for; matrix products, arithmetic and copies ran while one was open for 5% of the time, Pallas kernels for 0%

profile of v1, /device:TPU:0, one launch (start us, length us, event | category | flops | bytes accessed | tf_op | source)
XLA Modules:
  0.0 1187.9 jit_solution(7275630329626975454)
XLA Ops:
  10.7 6.2 gather_fusion.1
  20.8 96.5 %all-reduce.8.cloned.1.call-done = (f32[512,1024]{1,0:T(8,128)}, f32[128,512]{0,1:T(8,128)}) async-done(((f32[512,1024]{1,0:T(8,128)}, f32[128,512]{0,1:T(8,128)}), (f32[512,1024]{1,0:T(8,128)}, f32[128,512]{0,1:T(8,128)})) %all-reduce.8.cloned.1.call-update) | async-done | bytes 2359312 | tf_op jit(solution)/shard_map/psum | solution.py:35
  122.5 118.5 %all-reduce.6.cloned.1.call-done = f32[512,512]{1,0:T(8,128)} async-done(((f32[512,512]{1,0:T(8,128)}), f32[512,512]{1,0:T(8,128)}) %all-reduce.6.cloned.1.call-update) | async-done | bytes 1048592 | tf_op jit(solution)/shard_map/psum | solution.py:37
  244.5 2.4 convolution_subtract_fusion.9
  246.9 45.8 %all-gather.13.cloned.1.call-done = f32[512,512]{0,1:T(8,128)} async-done(((f32[512,64]{0,1:T(8,128)}), f32[512,512]{0,1:T(8,128)}) %all-gather.13.cloned.1.call-update) | async-done | bytes 1048592 | tf_op jit(solution)/shard_map/all_gather | solution.py:61
  292.7 2.7 fusion.8
  297.5 44.0 %all-gather.15.cloned.1.call-done = f32[512,512]{0,1:T(8,128)} async-done(((f32[512,64]{0,1:T(8,128)}), f32[512,512]{0,1:T(8,128)}) %all-gather.15.cloned.1.call-update) | async-done | bytes 1048592 | tf_op jit(solution)/shard_map/all_gather | solution.py:61
  341.5 2.7 fusion.9
  346.3 44.0 %all-gather.17.cloned.1.call-done = f32[512,512]{0,1:T(8,128)} async-done(((f32[512,64]{0,1:T(8,128)}), f32[512,512]{0,1:T(8,128)}) %all-gather.17.cloned.1.call-update) | async-done | bytes 1048592 | tf_op jit(solution)/shard_map/all_gather | solution.py:61
  390.3 2.7 fusion.10
  395.1 44.0 %all-gather.19.cloned.1.call-done = f32[512,512]{0,1:T(8,128)} async-done(((f32[512,64]{0,1:T(8,128)}), f32[512,512]{0,1:T(8,128)}) %all-gather.19.cloned.1.call-update) | async-done | bytes 1048592 | tf_op jit(solution)/shard_map/all_gather | solution.py:61
  439.1 2.7 fusion.11
  443.9 44.1 %all-gather.21.cloned.1.call-done = f32[512,512]{0,1:T(8,128)} async-done(((f32[512,64]{0,1:T(8,128)}), f32[512,512]{0,1:T(8,128)}) %all-gather.21.cloned.1.call-update) | async-done | bytes 1048592 | tf_op jit(solution)/shard_map/all_gather | solution.py:61
  488.0 2.7 fusion.12
  493.1 43.8 %all-gather.23.cloned.1.call-done = f32[512,512]{0,1:T(8,128)} async-done(((f32[512,64]{0,1:T(8,128)}), f32[512,512]{0,1:T(8,128)}) %all-gather.23.cloned.1.call-update) | async-done | bytes 1048592 | tf_op jit(solution)/shard_map/all_gather | solution.py:61
  536.8 2.7 fusion.13
  541.6 44.1 %all-gather.25.cloned.1.call-done = f32[512,512]{0,1:T(8,128)} async-done(((f32[512,64]{0,1:T(8,128)}), f32[512,512]{0,1:T(8,128)}) %all-gather.25.cloned.1.call-update) | async-done | bytes 1048592 | tf_op jit(solution)/shard_map/all_gather | solution.py:61
  585.7 2.7 fusion.14
  590.5 44.0 %all-gather.27.cloned.1.call-done = f32[512,512]{0,1:T(8,128)} async-done(((f32[512,64]{0,1:T(8,128)}), f32[512,512]{0,1:T(8,128)}) %all-gather.27.cloned.1.call-update) | async-done | bytes 1048592 | tf_op jit(solution)/shard_map/all_gather | solution.py:61
  634.5 2.7 fusion.15
  638.9 9.2 copy.17
  648.0 8.8 gather_fusion
  656.8 4.7 fusion
  661.5 5.4 copy.18
  668.2 15.2 %all-gather.29.cloned.1.call-done = f32[512,512]{0,1:T(8,128)} async-done(((f32[512,64]{0,1:T(8,128)}), f32[512,512]{0,1:T(8,128)}) %all-gather.29.cloned.1.call-update) | async-done | bytes 1048592 | tf_op jit(solution)/shard_map/all_gather | solution.py:64
  683.4 2.5 convolution_convert_fusion
  686.0 123.5 %all-reduce.10.cloned.1.call-done = (bf16[512,1024]{1,0:T(8,128)(2,1)}, bf16[512,1024]{1,0:T(8,128)(2,1)}) async-done(((bf16[512,1024]{1,0:T(8,128)(2,1)}, bf16[512,1024]{1,0:T(8,128)(2,1)}), (bf16[512,1024]{1,0:T(8,128)(2,1)}, bf16[512,1024]{1,0:T(8,128)(2,1)})) %all-reduce.10.cloned.1.call-update) | async-done | bytes 2097168 | tf_op jit(solution)/shard_map/psum | solution.py:11
  809.5 2.9 fusion.2
  812.4 4.8 fusion.16
  817.2 323.2 %all-gather.11.cloned.1.call-done = f32[16,2048,512]{2,1,0:T(8,128)} async-done(((f32[1,2048,512]{2,1,0:T(8,128)}), f32[16,2048,512]{2,1,0:T(8,128)}) %all-gather.11.cloned.1.call-update) | async-done | bytes 67108880 | tf_op jit(solution)/shard_map/all_gather | solution.py:40
  1140.4 23.1 %reduce_sum.18 = f32[2048,512]{1,0:T(8,128)} reduce(f32[16,2048,512]{2,1,0:T(8,128)} %all-gather.11.cloned.1.call-done, f32[]{:T(128)} %constant.45.clone.1), dimensions={0}, to_apply=%region_0.1 | reduce | flops 15728640 | bytes 71303168
  1163.5 17.8 %convolution_subtract_fusion = f32[2048,1024]{1,0:T(8,128)} fusion(f32[2048,1024]{1,0:T(8,128)} %param.3, f32[2048,512]{1,0:T(8,128)} %reduce_sum.18, f32[512,1024]{1,0:T(8,128)S(1)} %copy-done.2), kind=kOutput, calls=%fused_computation.7 | convolution fusion | flops 12886999040 | bytes 23068672 | tf_op jit(solution)/shard_map/dot_general | solution.py:70
  (65 shorter events, 33.4 us)
Async XLA Ops:
  7.2 110.2 %all-reduce.8.cloned.1.call-start = ((), (), s32[]{:S(2)}) async-start(), calls=%async_computation.11 | async-start | bytes 4718592 | tf_op jit(solution)/shard_map/psum | solution.py:35
  20.7 220.2 %all-reduce.6.cloned.1.call-start = ((), (), s32[]{:S(2)}) async-start(), calls=%async_computation.1 | async-start | bytes 2097152 | tf_op jit(solution)/shard_map/psum | solution.py:37
  122.4 170.4 %all-gather.13.cloned.1.call-start = ((), (), s32[]{:S(2)}) async-start(), calls=%async_computation.2 | async-start | bytes 1179648 | tf_op jit(solution)/shard_map/all_gather | solution.py:61
  241.0 54.5 %copy-start = (f32[512,512]{1,0:T(8,128)S(1)}, f32[512,512]{1,0:T(8,128)}, u32[]{:S(2)}) copy-start(f32[512,512]{1,0:T(8,128)} %all-reduce.6.cloned.1.call-done) | copy-start | bytes 3145732
  244.5 97.0 %all-gather.15.cloned.1.call-start = ((), (), s32[]{:S(2)}) async-start(), calls=%async_computation.3 | async-start | bytes 1179648 | tf_op jit(solution)/shard_map/all_gather | solution.py:61
  295.4 94.9 %all-gather.17.cloned.1.call-start = ((), (), s32[]{:S(2)}) async-start(), calls=%async_computation.4 | async-start | bytes 1179648 | tf_op jit(solution)/shard_map/all_gather | solution.py:61
  344.2 94.9 %all-gather.19.cloned.1.call-start = ((), (), s32[]{:S(2)}) async-start(), calls=%async_computation.5 | async-start | bytes 1179648 | tf_op jit(solution)/shard_map/all_gather | solution.py:61
  393.0 95.0 %all-gather.21.cloned.1.call-start = ((), (), s32[]{:S(2)}) async-start(), calls=%async_computation.6 | async-start | bytes 1179648 | tf_op jit(solution)/shard_map/all_gather | solution.py:61
  441.8 95.1 %all-gather.23.cloned.1.call-start = ((), (), s32[]{:S(2)}) async-start(), calls=%async_computation.7 | async-start | bytes 1179648 | tf_op jit(solution)/shard_map/all_gather | solution.py:61
  490.6 146.6 %copy-start.1 = (f32[512,1024]{1,0:T(8,128)S(1)}, f32[512,1024]{1,0:T(8,128)}, u32[]{:S(2)}) copy-start(f32[512,1024]{1,0:T(8,128)} %get-tuple-element.4) | copy-start | bytes 6291460
  490.6 95.1 %all-gather.25.cloned.1.call-start = ((), (), s32[]{:S(2)}) async-start(), calls=%async_computation.8 | async-start | bytes 1179648 | tf_op jit(solution)/shard_map/all_gather | solution.py:61
  539.5 95.0 %all-gather.27.cloned.1.call-start = ((), (), s32[]{:S(2)}) async-start(), calls=%async_computation.9 | async-start | bytes 1179648 | tf_op jit(solution)/shard_map/all_gather | solution.py:61
  588.4 95.0 %all-gather.29.cloned.1.call-start = ((), (), s32[]{:S(2)}) async-start(), calls=%async_computation.10 | async-start | bytes 1179648 | tf_op jit(solution)/shard_map/all_gather | solution.py:64
  637.2 172.3 %all-reduce.10.cloned.1.call-start = ((), (), s32[]{:S(2)}) async-start(), calls=%async_computation.12 | async-start | bytes 4194304 | tf_op jit(solution)/shard_map/psum | solution.py:11
  638.8 501.6 %all-gather.11.cloned.1.call-start = ((), (), s32[]{:S(2)}) async-start(), calls=%async_computation | async-start | bytes 71303168 | tf_op jit(solution)/shard_map/all_gather | solution.py:40
  666.9 0.7 copy-start.5
  666.9 16.5 %copy-start.4 = (f32[128,512]{0,1:T(8,128)S(1)}, f32[128,512]{0,1:T(8,128)}, u32[]{:S(2)}) copy-start(f32[128,512]{0,1:T(8,128)} %get-tuple-element.5) | copy-start | bytes 786436
  683.4 129.0 %copy-start.3 = (f32[512,512]{0,1:T(8,128)S(1)}, f32[512,512]{0,1:T(8,128)}, u32[]{:S(2)}) copy-start(f32[512,512]{0,1:T(8,128)} %all-gather.29.cloned.1.call-done) | copy-start | bytes 3145732
  817.2 346.4 %copy-start.2 = (f32[512,1024]{1,0:T(8,128)S(1)}, f32[512,1024]{1,0:T(8,128)}, u32[]{:S(2)}) copy-start(f32[512,1024]{1,0:T(8,128)} %fusion.16) | copy-start | bytes 6291460
Sparse Core Ops, SparseCore 0:
  20.9 96.4 all-reduce.7
  122.5 118.4 all-reduce.5
  244.6 48.0 all-gather.12
  295.5 45.9 all-gather.14
  344.3 45.9 all-gather.16
  393.1 45.9 all-gather.18
  442.0 45.9 all-gather.20
  490.9 45.9 all-gather.22
  539.7 45.9 all-gather.24
  588.5 45.9 all-gather.26
  637.4 45.9 all-gather.28
  685.8 123.6 all-reduce.9
  811.2 329.1 all-gather.10
